TPU v7x, 256 devices: a whole 4x4x8 slice. The times are simulated.
256 devices in a mesh: seq: 32 (over x, y, core), head: 8 (over z).
Axes of the slice: x: 4, y: 4, z: 8, core: 2. Of those that a mesh axis runs over, the one named last changes fastest.
Arguments:
- projected: bfloat16 [49152, 6912], P(('seq', 'head')), may hold values from -10 to 10
- segment_ids: int32 [49152], replicated, may hold values from 0 to 63, never falling along the last dimension, each value on 1 to 1536 neighbouring positions
- widths: int32 [64], replicated, may hold values from 16 to 64
Outputs:
- attended: bfloat16 [49152, 2304], P(('seq', 'head'))
Inputs may be any that keep to these rules, and one draw needn't show every extreme that they name: `segment_ids`: ids never fall along the sequence; each of the 64 samples covers 1 to 1536 consecutive positions and some sample covers exactly 1536.
All inputs are finite; a program needn't handle non-finite values.
Results may differ from a plain program's by a relative error of at most 0.0088.
Values may be sent and summed in bfloat16 or wider, within the bound.
No kernel may reach another device: no remote copies, remote signals or barrier semaphores. Data moves between devices by JAX's collectives and lax.ppermute only.
A program may use at most 128 MiB of HBM per device.

v0:
```python
import math

import jax
import jax.numpy as jnp
from jax import lax
from jax.sharding import PartitionSpec as P

D = 2304
HEADS = 24


masked_score = -1e30


def with_halo(shard, sides, width):
    for axis, dim in sides:
        size, length = (lax.axis_size(axis), shard.shape[dim])
        up = [(i, (i + 1) % size) for i in range(size - 1)]
        down = [(j, i) for i, j in up]
        last = lax.slice_in_dim(shard, length - width, length, axis=dim)
        first = lax.slice_in_dim(shard, 0, width, axis=dim)
        before = lax.ppermute(last, axis, up)
        after = lax.ppermute(first, axis, down)
        shard = jnp.concatenate([before, shard, after], axis=dim)
    return shard


def shortened(shard):

    def short(part):
        return part.astype(jnp.bfloat16) if part.dtype == jnp.float32 else part

    return jax.tree.map(short, shard)


def rotate(head_vals, row_pos, col_pos):
    quarter = head_vals.shape[-1] // 4
    frequency = 10000.0 ** (-jnp.arange(quarter, dtype=jnp.float32) / quarter)

    def turn(half_vals, place):
        angles = place.astype(jnp.float32)[:, None] * frequency[None, :]
        cosine = jnp.cos(angles)[:, None, :]
        sine_part = jnp.sin(angles)[:, None, :]
        first_half = half_vals[..., :quarter]
        second = half_vals[..., quarter:]
        return jnp.concatenate(
            [first_half * cosine - second * sine_part, first_half * sine_part + second * cosine],
            axis=-1,
        )

    middle = 2 * quarter
    return jnp.concatenate(
        [turn(head_vals[..., :middle], row_pos), turn(head_vals[..., middle:], col_pos)], axis=-1
    )


def starts_of(segment_ids):
    length = segment_ids.shape[0]
    indices = jnp.arange(length, dtype=jnp.int32)
    before = jnp.concatenate([jnp.full((1,), -1, jnp.int32), segment_ids[:-1]])
    return lax.cummax(jnp.where(segment_ids != before, indices, 0), axis=0)


def block_scores(q_rows, k_rows, q_ids, k_ids, scaling):
    scores = (
        lax.dot_general(
            q_rows, k_rows, (((1,), (1,)), ((), ())), preferred_element_type=jnp.float32
        )
        * scaling
    )
    same_seg = q_ids[:, None] == k_ids[None, :]
    return (jnp.where(same_seg, scores, masked_score), same_seg)


def dense_rows(q_rows, k_all, v_all, q_ids, k_ids, scaling):
    scores, same_seg = block_scores(q_rows, k_all, q_ids, k_ids, scaling)
    row_max = jnp.max(scores, axis=1, keepdims=True)
    weights = jnp.where(same_seg, jnp.exp(scores - row_max), 0.0)
    totals = jnp.sum(weights, axis=1, keepdims=True)
    blended = jnp.dot(weights.astype(jnp.bfloat16), v_all, preferred_element_type=jnp.float32)
    return (blended / totals).astype(jnp.bfloat16)


def attend(queries, key_rows, values, query_seg, key_seg):
    shard_rows, head_count, head_size = queries.shape
    block_rows = min(512, shard_rows)
    scaling = 1.0 / math.sqrt(head_size)

    def one_block(number):
        start_row = number * block_rows
        q_blk = lax.dynamic_slice_in_dim(queries, start_row, block_rows, 0)
        q_ids = lax.dynamic_slice_in_dim(query_seg, start_row, block_rows, 0)
        outputs = []
        for head_num in range(head_count):
            outputs.append(
                dense_rows(
                    q_blk[:, head_num],
                    key_rows[:, head_num],
                    values[:, head_num],
                    q_ids,
                    key_seg,
                    scaling,
                )
            )
        return jnp.stack(outputs, axis=1)

    results = lax.map(one_block, jnp.arange(shard_rows // block_rows, dtype=jnp.int32))
    return results.reshape(shard_rows, head_count, head_size)


def body(projected, segment_ids, widths):
    tok_dev = projected.shape[0]
    group_size = lax.axis_size("head")
    shard_rows = tok_dev * group_size
    head_size = D // HEADS
    local_heads = HEADS // group_size
    seq_index = lax.axis_index("seq")
    head_index = lax.axis_index("head")
    first_tok = (seq_index * group_size + head_index) * tok_dev
    starts = starts_of(segment_ids)
    own_seg = lax.dynamic_slice_in_dim(segment_ids, first_tok, tok_dev, 0)
    own_start = lax.dynamic_slice_in_dim(starts, first_tok, tok_dev, 0)
    offset = first_tok + jnp.arange(tok_dev, dtype=jnp.int32) - own_start
    sample_ids = jnp.arange(widths.shape[0], dtype=jnp.int32)
    width_tok = jnp.sum(
        jnp.where(own_seg[:, None] == sample_ids[None, :], widths[None, :], 0), axis=1
    )
    row_pos = offset // width_tok
    col_pos = offset % width_tok
    qkv_parts = projected.reshape(tok_dev, 3, HEADS, head_size)
    q_rot = rotate(qkv_parts[:, 0].astype(jnp.float32), row_pos, col_pos).astype(jnp.bfloat16)
    k_rot = rotate(qkv_parts[:, 1].astype(jnp.float32), row_pos, col_pos).astype(jnp.bfloat16)
    stacked = jnp.stack([q_rot, k_rot, qkv_parts[:, 2]], axis=1)
    stacked = stacked.reshape(tok_dev, 3, group_size, local_heads, head_size)
    query_seg = lax.dynamic_slice_in_dim(segment_ids, seq_index * shard_rows, shard_rows, 0)
    no_sample = jnp.full((shard_rows,), -1, jnp.int32)
    seg_pad = jnp.concatenate([no_sample, segment_ids, no_sample], axis=0)
    key_seg = lax.dynamic_slice_in_dim(seg_pad, seq_index * shard_rows, 3 * shard_rows, 0)
    qkv_part = lax.all_to_all(stacked, "head", split_axis=2, concat_axis=0, tiled=True)
    key_value = qkv_part[:, 1:]
    widened = with_halo(key_value, (("seq", 0),), qkv_part.shape[0])
    attended_heads = attend(
        qkv_part[:, 0, 0], widened[:, 0, 0], widened[:, 1, 0], query_seg, key_seg
    )
    returned = lax.all_to_all(
        shortened(attended_heads), "head", split_axis=0, concat_axis=1, tiled=True
    ).astype(attended_heads.dtype)
    return returned.reshape(tok_dev, HEADS * head_size)


def solution(mesh):
    in_specs = (P(("seq", "head"), None), P(), P())
    out_specs = P(("seq", "head"), None)
    return jax.shard_map(body, mesh=mesh, in_specs=in_specs, out_specs=out_specs, check_vma=False)
```

profile of v0, /device:TPU:20, one launch (start us, length us, event | category | flops | bytes accessed | tf_op | source)
XLA Modules:
  0.0 284.5 jit_solution(3814066336356876828)
XLA Ops:
  0.0 0.8 dynamic_slice.25
  0.8 1.1 select_bitcast_fusion
  3.0 0.8 copy.36
  3.8 4.8 %copy.34 = bf16[192,6912]{0,1:T(8,128)(2,1)S(1)} copy(bf16[192,6912]{1,0:T(8,128)(2,1)} %param.5) | data formatting | bytes 5308416 | tf_op args[0]
  9.2 0.9 fusion.62
  11.1 0.7 pad_maximum_fusion.1
  12.1 90.4 %all_to_all.33 = bf16[192,3,8,3,96]{0,4,3,1,2:T(8,128)(2,1)S(1)} all-to-all(bf16[192,3,8,3,96]{0,4,3,1,2:T(8,128)(2,1)S(1)} %copy.39), channel_id=1, replica_groups=mesh['seq'=32,'head'=8] {'head'}, dimensions={2} | all-to-all | bytes 5308416 | tf_op jit(solution)/shard_map/all_to_all | solution.py:139
  102.5 2.2 copy.40
  104.7 4.1 %all_to_all.27 = bf16[1536,3,1,3,96]{0,4,3,1,2:T(8,128)(2,1)} reshape(bf16[8,192,3,1,3,96]{1,0,5,4,2,3:T(8,128)(2,1)S(1)} %copy.40) | data formatting | bytes 5308416 | tf_op jit(solution)/shard_map/all_to_all | solution.py:139
  108.8 1.6 slice.133
  110.4 1.9 collective-permute-start
  112.3 3.6 %collective-permute-start.1 = (bf16[1536,2,1,3,96]{0,4,3,1,2:T(8,128)(2,1)S(1)}, bf16[1536,2,1,3,96]{0,4,3,1,2:T(8,128)(2,1)}, u32[]{:S(2)}, u32[]{:S(2)}) collective-permute-start(bf16[1536,2,1,3,96]{0,4,3,1,2:T(8,128)(2,1)S(1)} %slice.133), channel_id=1, source_target_pairs={{8,0},{16,8},{24,16},{32,24},{40,32},{48,40},{56,48},{64,56},{72,6... | collective-permute-start | bytes 5308424 | tf_op jit(solution)/shard_map/ppermute | solution.py:23
  116.0 0.8 dynamic_slice.22
  116.8 1.5 fusion.61
  118.2 2.2 slice_bitcast_fusion.4
  120.4 13.8 %collective-permute-done = bf16[1536,2,1,3,96]{0,4,3,1,2:T(8,128)(2,1)S(1)} collective-permute-done((bf16[1536,2,1,3,96]{0,4,3,1,2:T(8,128)(2,1)S(1)}, bf16[1536,2,1,3,96]{0,4,3,1,2:T(8,128)(2,1)S(1)}, u32[]{:S(2)}, u32[]{:S(2)}) %collective-permute-start) | collective-permute-done | bytes 1769504 | tf_op jit(solution)/shard_map/ppermute | solution.py:22
  134.2 1.8 collective-permute-done.1
  136.0 2.4 pad_maximum_fusion
  138.4 1.8 slice_bitcast_fusion
  140.2 97.8 %while.10 = (s32[]{:T(128)}, bf16[3,512,3,96]{1,3,2,0:T(8,128)(2,1)S(1)}, s32[3]{0:T(128)S(1)}, s32[1536]{0:T(1024)S(1)}, s32[4608]{0:T(1024)}, /*index=5*/bf16[...) while((s32[]{:T(128)}, ...), condition=%wide.region_11.12_spmd, body=%wide.region_4.11_spmd.sunk | while | flops 2799301632 | bytes 157868512 | solution.py:107
  141.7 6.5 %fusion.89 = (f32[512]{0:T(512)S(1)}, f32[512,4608]{1,0:T(8,128)}) fusion(bf16[4608,3,96]{0,2,1:T(8,128)(2,1)} %get-tuple-element.199, bf16[1536,3,96]{0,2,1:T(8,128)(2,1)} %get-tuple-element.198, s32[]{:T(128)S(6)} %select_n.123, s32[]{:T(128)S(6)} %add.94, s32[4608]{0:T(1024)} %get-tuple-element.197, s32[512]{0:T(512)S(1)} %dynamic_slice.48), kind=kOutput, calls=%fused_computation.91.clone.1 | convolution fusion | flops 462421504 | bytes 10444808 | tf_op jit(solution)/shard_map/while/body/eval_jaxpr/dot_general | solution.py:66
  148.1 6.5 %fusion.88 = (f32[512]{0:T(512)S(1)}, f32[512,4608]{1,0:T(8,128)}) fusion(bf16[4608,3,96]{0,2,1:T(8,128)(2,1)} %get-tuple-element.199, bf16[1536,3,96]{0,2,1:T(8,128)(2,1)} %get-tuple-element.198, s32[]{:T(128)S(6)} %select_n.123, s32[4608]{0:T(1024)S(1)} %copy-done.2, s32[512]{0:T(512)S(1)} %dynamic_slice.48), kind=kOutput, calls=%fused_computation.90.clone.1 | convolution fusion | flops 462421504 | bytes 10442756 | tf_op jit(solution)/shard_map/while/body/eval_jaxpr/dot_general | solution.py:66
  154.7 3.0 %fusion.87 = (f32[512]{0:T(512)S(1)}, f32[512,4608]{1,0:T(8,128)S(1)}) fusion(bf16[4608,3,96]{0,2,1:T(8,128)(2,1)} %get-tuple-element.199, bf16[1536,3,96]{0,2,1:T(8,128)(2,1)} %get-tuple-element.198, s32[]{:T(128)S(6)} %select_n.123, s32[]{:T(128)S(6)} %add.93, s32[4608]{0:T(1024)} %get-tuple-element.197, s32[512]{0:T(512)S(1)} %dynamic_slice.48), kind=kOutput, calls=%fused_computation.89.clone.1 | convolution fusion | flops 462421504 | bytes 10444808 | tf_op jit(solution)/shard_map/while/body/eval_jaxpr/dot_general | solution.py:66
  157.7 0.9 copy-done
  158.7 8.5 %fusion.90 = (f32[512]{0:T(512)S(1)}, f32[512]{0:T(512)S(1)}, f32[512]{0:T(512)S(1)}) fusion(f32[512,4608]{1,0:T(8,128)S(1)} %copy-done, f32[512]{0:T(512)S(1)} %get-tuple-element.159, s32[4608]{0:T(1024)S(1)} %copy-done.3, s32[512]{0:T(512)S(1)} %dynamic_slice.48, f32[512,4608]{1,0:T(8,128)} %get-tuple-element.160, f32[512]{0:T(512)S(1)} %get-tuple-element.161, ...), kind=kLoop, calls=%fused_computation.6.clone.1 | loop fusion | flops 23591424 | bytes 28344320 | tf_op jit(solution)/shard_map/while/body/eval_jaxpr/reduce_sum | solution.py:79
  167.2 1.8 fusion.93
  169.1 1.8 fusion.92
  170.9 1.8 fusion.91
  174.3 6.5 %fusion.89 = (f32[512]{0:T(512)S(1)}, f32[512,4608]{1,0:T(8,128)}) fusion(bf16[4608,3,96]{0,2,1:T(8,128)(2,1)} %get-tuple-element.199, bf16[1536,3,96]{0,2,1:T(8,128)(2,1)} %get-tuple-element.198, s32[]{:T(128)S(6)} %select_n.123, s32[]{:T(128)S(6)} %add.94, s32[4608]{0:T(1024)} %get-tuple-element.197, s32[512]{0:T(512)S(1)} %dynamic_slice.48), kind=kOutput, calls=%fused_computation.91.clone.1 | convolution fusion | flops 462421504 | bytes 10444808 | tf_op jit(solution)/shard_map/while/body/eval_jaxpr/dot_general | solution.py:66
  180.7 6.5 %fusion.88 = (f32[512]{0:T(512)S(1)}, f32[512,4608]{1,0:T(8,128)}) fusion(bf16[4608,3,96]{0,2,1:T(8,128)(2,1)} %get-tuple-element.199, bf16[1536,3,96]{0,2,1:T(8,128)(2,1)} %get-tuple-element.198, s32[]{:T(128)S(6)} %select_n.123, s32[4608]{0:T(1024)S(1)} %copy-done.2, s32[512]{0:T(512)S(1)} %dynamic_slice.48), kind=kOutput, calls=%fused_computation.90.clone.1 | convolution fusion | flops 462421504 | bytes 10442756 | tf_op jit(solution)/shard_map/while/body/eval_jaxpr/dot_general | solution.py:66
  187.3 3.0 %fusion.87 = (f32[512]{0:T(512)S(1)}, f32[512,4608]{1,0:T(8,128)S(1)}) fusion(bf16[4608,3,96]{0,2,1:T(8,128)(2,1)} %get-tuple-element.199, bf16[1536,3,96]{0,2,1:T(8,128)(2,1)} %get-tuple-element.198, s32[]{:T(128)S(6)} %select_n.123, s32[]{:T(128)S(6)} %add.93, s32[4608]{0:T(1024)} %get-tuple-element.197, s32[512]{0:T(512)S(1)} %dynamic_slice.48), kind=kOutput, calls=%fused_computation.89.clone.1 | convolution fusion | flops 462421504 | bytes 10444808 | tf_op jit(solution)/shard_map/while/body/eval_jaxpr/dot_general | solution.py:66
  190.3 0.9 copy-done
  191.3 8.5 %fusion.90 = (f32[512]{0:T(512)S(1)}, f32[512]{0:T(512)S(1)}, f32[512]{0:T(512)S(1)}) fusion(f32[512,4608]{1,0:T(8,128)S(1)} %copy-done, f32[512]{0:T(512)S(1)} %get-tuple-element.159, s32[4608]{0:T(1024)S(1)} %copy-done.3, s32[512]{0:T(512)S(1)} %dynamic_slice.48, f32[512,4608]{1,0:T(8,128)} %get-tuple-element.160, f32[512]{0:T(512)S(1)} %get-tuple-element.161, ...), kind=kLoop, calls=%fused_computation.6.clone.1 | loop fusion | flops 23591424 | bytes 28344320 | tf_op jit(solution)/shard_map/while/body/eval_jaxpr/reduce_sum | solution.py:79
  199.8 1.8 fusion.93
  201.7 1.8 fusion.92
  203.5 1.8 fusion.91
  206.9 6.5 %fusion.89 = (f32[512]{0:T(512)S(1)}, f32[512,4608]{1,0:T(8,128)}) fusion(bf16[4608,3,96]{0,2,1:T(8,128)(2,1)} %get-tuple-element.199, bf16[1536,3,96]{0,2,1:T(8,128)(2,1)} %get-tuple-element.198, s32[]{:T(128)S(6)} %select_n.123, s32[]{:T(128)S(6)} %add.94, s32[4608]{0:T(1024)} %get-tuple-element.197, s32[512]{0:T(512)S(1)} %dynamic_slice.48), kind=kOutput, calls=%fused_computation.91.clone.1 | convolution fusion | flops 462421504 | bytes 10444808 | tf_op jit(solution)/shard_map/while/body/eval_jaxpr/dot_general | solution.py:66
  213.4 6.5 %fusion.88 = (f32[512]{0:T(512)S(1)}, f32[512,4608]{1,0:T(8,128)}) fusion(bf16[4608,3,96]{0,2,1:T(8,128)(2,1)} %get-tuple-element.199, bf16[1536,3,96]{0,2,1:T(8,128)(2,1)} %get-tuple-element.198, s32[]{:T(128)S(6)} %select_n.123, s32[4608]{0:T(1024)S(1)} %copy-done.2, s32[512]{0:T(512)S(1)} %dynamic_slice.48), kind=kOutput, calls=%fused_computation.90.clone.1 | convolution fusion | flops 462421504 | bytes 10442756 | tf_op jit(solution)/shard_map/while/body/eval_jaxpr/dot_general | solution.py:66
  219.9 3.0 %fusion.87 = (f32[512]{0:T(512)S(1)}, f32[512,4608]{1,0:T(8,128)S(1)}) fusion(bf16[4608,3,96]{0,2,1:T(8,128)(2,1)} %get-tuple-element.199, bf16[1536,3,96]{0,2,1:T(8,128)(2,1)} %get-tuple-element.198, s32[]{:T(128)S(6)} %select_n.123, s32[]{:T(128)S(6)} %add.93, s32[4608]{0:T(1024)} %get-tuple-element.197, s32[512]{0:T(512)S(1)} %dynamic_slice.48), kind=kOutput, calls=%fused_computation.89.clone.1 | convolution fusion | flops 462421504 | bytes 10444808 | tf_op jit(solution)/shard_map/while/body/eval_jaxpr/dot_general | solution.py:66
  223.0 0.9 copy-done
  223.9 8.5 %fusion.90 = (f32[512]{0:T(512)S(1)}, f32[512]{0:T(512)S(1)}, f32[512]{0:T(512)S(1)}) fusion(f32[512,4608]{1,0:T(8,128)S(1)} %copy-done, f32[512]{0:T(512)S(1)} %get-tuple-element.159, s32[4608]{0:T(1024)S(1)} %copy-done.3, s32[512]{0:T(512)S(1)} %dynamic_slice.48, f32[512,4608]{1,0:T(8,128)} %get-tuple-element.160, f32[512]{0:T(512)S(1)} %get-tuple-element.161, ...), kind=kLoop, calls=%fused_computation.6.clone.1 | loop fusion | flops 23591424 | bytes 28344320 | tf_op jit(solution)/shard_map/while/body/eval_jaxpr/reduce_sum | solution.py:79
  232.4 1.8 fusion.93
  234.3 1.8 fusion.92
  236.2 1.8 fusion.91
  238.1 1.1 copy.47
  239.1 43.1 %all_to_all.34 = bf16[1536,3,96]{2,1,0:T(4,128)(2,1)S(1)} all-to-all(bf16[1536,3,96]{2,1,0:T(4,128)(2,1)S(1)} %bitcast.128), channel_id=1, replica_groups=mesh['seq'=32,'head'=8] {'head'}, dimensions={0} | all-to-all | bytes 1769472 | tf_op jit(solution)/shard_map/all_to_all | solution.py:145
  282.3 0.9 copy.49
  283.2 1.3 copy.45
  (81 shorter events, 5.3 us)
Async XLA Ops:
  3.8 5.3 %copy-start.6 = (s32[64]{0:T(128)S(1)}, s32[64]{0:T(128)}, u32[]{:S(2)}) copy-start(s32[64]{0:T(128)} %param.7) | copy-start | bytes 772
  110.4 23.8 %collective-permute-start = (bf16[1536,2,1,3,96]{0,4,3,1,2:T(8,128)(2,1)S(1)}, bf16[1536,2,1,3,96]{0,4,3,1,2:T(8,128)(2,1)S(1)}, u32[]{:S(2)}, u32[]{:S(2)}) collective-permute-start(bf16[1536,2,1,3,96]{0,4,3,1,2:T(8,128)(2,1)S(1)} %slice.133), channel_id=1, source_target_pairs={{0,8},{8,16},{16,24},{24,32},{32,40},{40,48},{48,56},{56,64},{64,7... | collective-permute-start | bytes 5308424 | tf_op jit(solution)/shard_map/ppermute | solution.py:22
  112.3 23.7 %collective-permute-start.1 = (bf16[1536,2,1,3,96]{0,4,3,1,2:T(8,128)(2,1)S(1)}, bf16[1536,2,1,3,96]{0,4,3,1,2:T(8,128)(2,1)}, u32[]{:S(2)}, u32[]{:S(2)}) collective-permute-start(bf16[1536,2,1,3,96]{0,4,3,1,2:T(8,128)(2,1)S(1)} %slice.133), channel_id=1, source_target_pairs={{8,0},{16,8},{24,16},{32,24},{40,32},{48,40},{56,48},{64,56},{72,6... | collective-permute-start | bytes 5308424 | tf_op jit(solution)/shard_map/ppermute | solution.py:23
  138.4 1.8 copy-start.1
  140.2 1.4 copy-start.4
  141.7 6.5 %copy-start.2 = (s32[4608]{0:T(1024)S(1)}, s32[4608]{0:T(1024)}, u32[]{:S(2)}) copy-start(s32[4608]{0:T(1024)} %get-tuple-element.197) | copy-start | bytes 55300 | tf_op jit(solution)/shard_map/while
  154.7 4.0 %copy-start = (f32[512,4608]{1,0:T(8,128)S(1)}, f32[512,4608]{1,0:T(8,128)}, u32[]{:S(2)}) copy-start(f32[512,4608]{1,0:T(8,128)} %get-tuple-element.158) | copy-start | bytes 28311556 | tf_op jit(solution)/shard_map/while
  154.7 4.0 %copy-start.3 = (s32[4608]{0:T(1024)S(1)}, s32[4608]{0:T(1024)}, u32[]{:S(2)}) copy-start(s32[4608]{0:T(1024)} %get-tuple-element.197) | copy-start | bytes 55300 | tf_op jit(solution)/shard_map/while
  158.7 10.4 %slice-start = ((s8[9437184]{0:T(1024)(128)(4,1)}), s8[4194304]{0:T(1024)(128)(4,1)S(1)}, s32[]{:S(2)}) async-start(s8[9437184]{0:T(1024)(128)(4,1)} %bitcast.124), calls=%async_computation.2 | async-start | bytes 8388608 | tf_op jit(solution)/shard_map/while
  158.7 10.4 %slice-start.1 = ((s8[9437184]{0:T(1024)(128)(4,1)}), s8[4194304]{0:T(1024)(128)(4,1)S(1)}, s32[]{:S(2)}) async-start(s8[9437184]{0:T(1024)(128)(4,1)} %bitcast.124), calls=%async_computation.3 | async-start | bytes 8388608 | tf_op jit(solution)/shard_map/while
  167.2 1.9 slice-start.2
  170.9 1.9 copy-start.5
  172.8 1.5 copy-start.4
  174.3 6.5 %copy-start.2 = (s32[4608]{0:T(1024)S(1)}, s32[4608]{0:T(1024)}, u32[]{:S(2)}) copy-start(s32[4608]{0:T(1024)} %get-tuple-element.197) | copy-start | bytes 55300 | tf_op jit(solution)/shard_map/while
  187.3 4.0 %copy-start = (f32[512,4608]{1,0:T(8,128)S(1)}, f32[512,4608]{1,0:T(8,128)}, u32[]{:S(2)}) copy-start(f32[512,4608]{1,0:T(8,128)} %get-tuple-element.158) | copy-start | bytes 28311556 | tf_op jit(solution)/shard_map/while
  187.3 4.0 %copy-start.3 = (s32[4608]{0:T(1024)S(1)}, s32[4608]{0:T(1024)}, u32[]{:S(2)}) copy-start(s32[4608]{0:T(1024)} %get-tuple-element.197) | copy-start | bytes 55300 | tf_op jit(solution)/shard_map/while
  191.3 10.4 %slice-start = ((s8[9437184]{0:T(1024)(128)(4,1)}), s8[4194304]{0:T(1024)(128)(4,1)S(1)}, s32[]{:S(2)}) async-start(s8[9437184]{0:T(1024)(128)(4,1)} %bitcast.124), calls=%async_computation.2 | async-start | bytes 8388608 | tf_op jit(solution)/shard_map/while
  191.3 10.4 %slice-start.1 = ((s8[9437184]{0:T(1024)(128)(4,1)}), s8[4194304]{0:T(1024)(128)(4,1)S(1)}, s32[]{:S(2)}) async-start(s8[9437184]{0:T(1024)(128)(4,1)} %bitcast.124), calls=%async_computation.3 | async-start | bytes 8388608 | tf_op jit(solution)/shard_map/while
  199.8 1.9 slice-start.2
  203.5 1.9 copy-start.5
  205.4 1.5 copy-start.4
  206.9 6.5 %copy-start.2 = (s32[4608]{0:T(1024)S(1)}, s32[4608]{0:T(1024)}, u32[]{:S(2)}) copy-start(s32[4608]{0:T(1024)} %get-tuple-element.197) | copy-start | bytes 55300 | tf_op jit(solution)/shard_map/while
  219.9 4.0 %copy-start = (f32[512,4608]{1,0:T(8,128)S(1)}, f32[512,4608]{1,0:T(8,128)}, u32[]{:S(2)}) copy-start(f32[512,4608]{1,0:T(8,128)} %get-tuple-element.158) | copy-start | bytes 28311556 | tf_op jit(solution)/shard_map/while
  219.9 4.0 %copy-start.3 = (s32[4608]{0:T(1024)S(1)}, s32[4608]{0:T(1024)}, u32[]{:S(2)}) copy-start(s32[4608]{0:T(1024)} %get-tuple-element.197) | copy-start | bytes 55300 | tf_op jit(solution)/shard_map/while
  223.9 10.4 %slice-start = ((s8[9437184]{0:T(1024)(128)(4,1)}), s8[4194304]{0:T(1024)(128)(4,1)S(1)}, s32[]{:S(2)}) async-start(s8[9437184]{0:T(1024)(128)(4,1)} %bitcast.124), calls=%async_computation.2 | async-start | bytes 8388608 | tf_op jit(solution)/shard_map/while
  223.9 10.4 %slice-start.1 = ((s8[9437184]{0:T(1024)(128)(4,1)}), s8[4194304]{0:T(1024)(128)(4,1)S(1)}, s32[]{:S(2)}) async-start(s8[9437184]{0:T(1024)(128)(4,1)} %bitcast.124), calls=%async_computation.3 | async-start | bytes 8388608 | tf_op jit(solution)/shard_map/while
  232.4 1.9 slice-start.2
  236.2 1.9 copy-start.5
where the time goes:
time: 287 us; the launch traced here: 285 us
  blocking collectives  134 us (47%)
  matrix products  64.6 us (23%)
  other arithmetic  34.4 us (12%)
  local copies, waits for them, and re-layouts  28.2 us (10%)
  waiting for transfers between devices  15.6 us (5%)
  starting transfers between devices  5.56 us (2%)
    all_to_all x1, blocking collectives, body(): lax.all_to_all(stacked, 'head', split_axis=2, concat_axis=0, tiled=True)  90.4 us
    dot_general x9, matrix products, block_scores(): lax.dot_general(q_rows, k_rows, (((1,), (1,)), ((), ())), preferred_eleme...  48.1 us
    all_to_all x1, blocking collectives, body(): lax.all_to_all(shortened(attended_heads), 'head', split_axis=0, concat_ax...  43.1 us
    reduce_sum x3, other arithmetic, dense_rows(): totals = jnp.sum(weights, axis=1, keepdims=True)  25.5 us
    dot_general x9, matrix products, dense_rows(): jnp.dot(weights.astype(jnp.bfloat16), v_all, preferred_element_type=jnp.f...  16.5 us
    ppermute x1, waiting for transfers between devices, with_halo(): before = lax.ppermute(last, axis, up)  13.8 us
    all_to_all x2, local copies, waits for them, and re-layouts, body(): lax.all_to_all(stacked, 'head', split_axis=2, concat_axis=0, tiled=True)  6.32 us
  transfers between devices with their start and end apart: 2, of which 2 were waited for; matrix products, arithmetic and copies ran while one was open for 2% of the time, Pallas kernels for 0%

commit v1 on v0

v1 whole, which is shorter than its diff:
```python
import math

import jax
import jax.numpy as jnp
import numpy as np
from jax import lax
from jax.experimental import pallas as pl
from jax.experimental.pallas import tpu as pltpu
from jax.sharding import PartitionSpec as P

D = 2304
HEADS = 24
HD = 96
TOKENS = 49152
SAMPLES = 64
GROUP = 8
SEQ = 32
OWN = 192
SHARD = OWN * GROUP
LANES = 128
SEG_ROWS = TOKENS // LANES
SHARD_ROWS = SHARD // LANES

KV_LANES = 5 * LANES
Q_LANES = 2 * LANES
CODE = 64
BITS = 6
ONE = CODE + 2 * BITS
BIG = float(2**20)
BQ = OWN
BK = 256
MAX_BLOCKS = 14
WINDOW = 3 * SHARD
OUT_ROWS = 2 * OWN + OWN // 4
SCALE = math.log2(math.e) / math.sqrt(HD)


def lane_iota(shape, dtype=jnp.int32):
    return lax.broadcasted_iota(dtype, shape, len(shape) - 1)


def turned(x, amount):
    amount %= LANES
    return x if amount == 0 else pltpu.roll(x, amount, 1)


def pack_kernel(x_ref, seg_ref, widths_ref, freq_ref, kv_ref, q_ref, cos_ref, sin_ref, code_ref):
    device = lax.axis_index("seq") * GROUP + lax.axis_index("head")
    first_tok = device * OWN
    first_row = jnp.maximum(first_tok // LANES - SHARD_ROWS, 0)
    rows = lax.broadcasted_iota(jnp.int32, (OWN, 1), 0)
    lanes = lane_iota((1, LANES))
    window = SHARD_ROWS + 2
    own = jnp.zeros((OWN, LANES), jnp.float32)
    for r in range(window):
        ids = seg_ref[pl.ds(first_row + r, 1), :].astype(jnp.float32)
        place = (first_row + r) * LANES + lanes - first_tok
        own = own + jnp.where(place == rows, ids, 0.0)
    own = jnp.sum(own, axis=1, keepdims=True)
    before = jnp.zeros((OWN, LANES), jnp.float32)
    for r in range(window):
        ids = seg_ref[pl.ds(first_row + r, 1), :].astype(jnp.float32)
        place = (first_row + r) * LANES + lanes - first_tok
        before = before + jnp.where((ids == own) & (place < rows), 1.0, 0.0)
    offset = jnp.sum(before, axis=1, keepdims=True)
    lane_f = lanes.astype(jnp.float32)
    width = jnp.sum(jnp.where(own == lane_f, widths_ref[...].astype(jnp.float32), 0.0), axis=1, keepdims=True)
    row_pos = jnp.floor((offset + 0.5) / width)
    col_pos = offset - row_pos * width
    angle = jnp.where(lanes < HD // 2, row_pos, col_pos) * freq_ref[...]
    first_half = (lanes % (HD // 2)) < HD // 4
    sine = jnp.sin(angle)
    cos_ref[...] = jnp.cos(angle)
    sin_ref[...] = jnp.where(first_half, -sine, sine)
    ids = own.astype(jnp.int32)
    shift = jnp.clip(jnp.where(lanes < CODE + BITS, lanes - CODE, lanes - CODE - BITS), 0, BITS - 1)
    bit = (ids >> shift) & 1
    code = jnp.where(lanes < CODE + BITS, 1 - bit, bit)
    code = jnp.where(lanes == ONE, 1, jnp.where((lanes >= CODE) & (lanes < ONE), code, 0))
    code_ref[...] = code.astype(jnp.float32).astype(jnp.bfloat16)

    step_rows = 32

    def step(i, carry):
        at = pl.ds(pl.multiple_of(i * step_rows, step_rows), step_rows)
        cos = cos_ref[at, :]
        sin = sin_ref[at, :]
        lane = lane_iota((step_rows, LANES))
        first = (lane % (HD // 2)) < HD // 4

        def tile(t):
            return x_ref[at, t * LANES : (t + 1) * LANES]

        def granules(base, count, target):
            t, g = base // LANES, base % LANES
            value = turned(tile(t), target - g)
            if g + 32 * count > LANES:
                cut = target + LANES - g
                value = jnp.where(lane < cut, value, turned(tile(t + 1), target - g))
            return value

        def rope(base):
            x = granules(base, 3, 0).astype(jnp.float32)
            other = jnp.where(first, pltpu.roll(x, LANES - HD // 4, 1), pltpu.roll(x, HD // 4, 1))
            return (x * cos + other * sin).astype(jnp.bfloat16)

        for z in range(GROUP):
            q0 = z * 3 * HD
            k0, v0 = D + q0, 2 * D + q0
            for h in range(3):
                kv_ref[z, at, h * LANES : (h + 1) * LANES] = jnp.where(
                    lane < HD, rope(k0 + h * HD), granules(v0 + 32 * h, 1, HD)
                )
            kv_ref[z, at, 3 * LANES : 4 * LANES] = jnp.where(
                lane < HD, granules(v0 + HD, 3, 0), granules(v0 + 2 * HD, 1, HD)
            )
            q2 = rope(q0 + 2 * HD)
            tail = jnp.where(lane < HD, code_ref[at, :], turned(q2, 32))
            kv_ref[z, at, 4 * LANES : 5 * LANES] = jnp.where(lane < CODE, granules(v0 + 2 * HD + 32, 2, 0), tail)
            q_ref[z, at, :LANES] = jnp.where(lane < HD, rope(q0), turned(q2, HD))
            q_ref[z, at, LANES:] = jnp.where(lane < HD, rope(q0 + HD), turned(q2, 64))
        return carry

    lax.fori_loop(0, OWN // step_rows, step, 0)


def pack(projected, seg_rows, widths_row, freq):
    vmem = pl.BlockSpec(memory_space=pltpu.VMEM)
    return pl.pallas_call(
        pack_kernel,
        out_shape=[
            jax.ShapeDtypeStruct((GROUP, OWN, KV_LANES), jnp.bfloat16),
            jax.ShapeDtypeStruct((GROUP, OWN, Q_LANES), jnp.bfloat16),
        ],
        in_specs=[vmem] * 4,
        out_specs=[vmem] * 2,
        scratch_shapes=[
            pltpu.VMEM((OWN, LANES), jnp.float32),
            pltpu.VMEM((OWN, LANES), jnp.float32),
            pltpu.VMEM((OWN, LANES), jnp.bfloat16),
        ],
        compiler_params=pltpu.CompilerParams(vmem_limit_bytes=40 * 1024 * 1024),
        name="pack",
    )(projected, seg_rows, widths_row, freq)


def attend_kernel(
    prev_ref, own_ref, next_ref, q_ref, seg_ref, out_ref, kv_ref, v0_ref, qa_ref, qc_ref, s_ref, m_ref, o0_ref, o12_ref, lo_ref, hi_ref
):
    shard = lax.axis_index("seq")
    lanes = lane_iota((1, LANES))

    def ids_of(index):
        return seg_ref[pl.ds(pl.multiple_of(index * SHARD_ROWS, 4), SHARD_ROWS), :].astype(jnp.float32)

    own_ids = ids_of(shard)
    prev_ids = jnp.where(shard > 0, ids_of(jnp.maximum(shard - 1, 0)), -1.0)
    next_ids = jnp.where(shard < SEQ - 1, ids_of(jnp.minimum(shard + 1, SEQ - 1)), -1.0)
    place = lax.broadcasted_iota(jnp.int32, (SHARD_ROWS, LANES), 0) * LANES + lane_iota((SHARD_ROWS, LANES))

    def total(x):
        return jnp.sum(jnp.sum(x, axis=0, keepdims=True), axis=1, keepdims=True)

    for b in range(GROUP):
        first = total(jnp.where(place == b * BQ, own_ids, 0.0))
        last = total(jnp.where(place == b * BQ + BQ - 1, own_ids, 0.0))
        low = total(jnp.where(own_ids < first, 1.0, 0.0) - jnp.where(prev_ids == first, 1.0, 0.0))
        high = total(jnp.where(own_ids <= last, 1.0, 0.0) + jnp.where(next_ids == last, 1.0, 0.0))
        lo_ref[b] = low[0, 0].astype(jnp.int32) + SHARD
        hi_ref[b] = high[0, 0].astype(jnp.int32) + SHARD

    chunk = LANES
    first_chunk = lo_ref[0] // chunk
    last_chunk = (hi_ref[GROUP - 1] + BK + chunk - 1) // chunk

    def copy_from(ref, number):
        begin = jnp.clip(first_chunk, number * SHARD_ROWS, (number + 1) * SHARD_ROWS)
        end = jnp.clip(last_chunk, number * SHARD_ROWS, (number + 1) * SHARD_ROWS)

        def move(i, carry):
            src = pl.ds(pl.multiple_of((i - number * SHARD_ROWS) * chunk, chunk), chunk)
            dst = pl.ds(pl.multiple_of(i * chunk, chunk), chunk)
            lane = lane_iota((chunk, LANES))
            parts = []
            for t in range(5):
                value = ref[src, t * LANES : (t + 1) * LANES]
                kv_ref[dst, t * LANES : (t + 1) * LANES] = value
                parts.append(value)
            v0 = jnp.where(lane < 32, turned(parts[0], 32), jnp.where(lane < 64, turned(parts[1], 64), turned(parts[2], 96)))
            v0_ref[dst, :] = jnp.where(lane < HD, v0, jnp.where(lane == HD, 1.0, 0.0).astype(jnp.bfloat16))
            return carry

        lax.fori_loop(begin, end, move, 0)

    copy_from(prev_ref, 0)
    copy_from(own_ref, 1)
    copy_from(next_ref, 2)

    def prepare(b, carry):
        at = pl.ds(pl.multiple_of(b * BQ, BQ), BQ)
        lane = lane_iota((BQ, LANES))
        zero = jnp.zeros((BQ, LANES), jnp.bfloat16)
        t4 = own_ref[at, 4 * LANES :]
        t5 = q_ref[at, :LANES]
        t6 = q_ref[at, LANES:]
        qa_ref[0, at, :] = jnp.where(lane < HD, t5, zero)
        qa_ref[1, at, :] = jnp.where(lane < HD, t6, zero)
        q2 = jnp.where(lane < 32, turned(t5, 32), jnp.where(lane < 64, turned(t6, 64), turned(t4, 96)))
        qa_ref[2, at, :] = jnp.where(lane < HD, q2, zero)
        other = (t4.astype(jnp.float32) - 1.0) * BIG
        qc_ref[at, :] = jnp.where((lane >= CODE) & (lane < ONE), other, 0.0).astype(jnp.bfloat16)
        return carry

    lax.fori_loop(0, GROUP, prepare, 0)

    def block(b, carry):
        lo, hi = lo_ref[b], hi_ref[b]
        start = lo // LANES * LANES
        count = (hi - start + BK - 1) // BK
        start = jnp.minimum(start, WINDOW - count * BK)
        at = pl.ds(pl.multiple_of(b * BQ, BQ), BQ)
        m_ref[...] = jnp.full_like(m_ref, -3.0e38)
        o0_ref[...] = jnp.zeros_like(o0_ref)
        o12_ref[...] = jnp.zeros_like(o12_ref)

        def scores(j, c):
            keys = pl.ds(pl.multiple_of(start + j * BK, LANES), BK)
            t4 = kv_ref[keys, 4 * LANES :]
            for h in range(3):
                k = jnp.concatenate([kv_ref[keys, h * LANES : (h + 1) * LANES], t4], axis=1)
                q = jnp.concatenate([qa_ref[h, at, :], qc_ref[at, :]], axis=1)
                s = lax.dot_general(q, k, (((1,), (1,)), ((), ())), preferred_element_type=jnp.float32)
                s_ref[j, h] = s
                top = s[:, :LANES]
                for t in range(1, BK // LANES):
                    top = jnp.maximum(top, s[:, t * LANES : (t + 1) * LANES])
                m_ref[h] = jnp.maximum(m_ref[h], top)
            return c

        lax.fori_loop(0, count, scores, 0)
        for h in range(3):
            m_ref[h] = jnp.broadcast_to(jnp.max(m_ref[h], axis=1, keepdims=True) * SCALE, (BQ, LANES))

        def blend(j, c):
            keys = pl.ds(pl.multiple_of(start + j * BK, LANES), BK)
            weights = []
            for h in range(3):
                m = jnp.concatenate([m_ref[h]] * (BK // LANES), axis=1)
                weights.append(jnp.exp2(s_ref[j, h] * SCALE - m).astype(jnp.bfloat16))
            o0_ref[...] += jnp.dot(weights[0], v0_ref[keys, :], preferred_element_type=jnp.float32)
            both = jnp.concatenate(weights[1:], axis=0)
            o12_ref[...] += jnp.dot(both, kv_ref[keys, 3 * LANES :], preferred_element_type=jnp.float32)
            return c

        lax.fori_loop(0, count, blend, 0)

        lane = lane_iota((BQ, LANES))
        o0 = o0_ref[...]
        o0 = o0 / o0[:, HD : HD + 1]
        o1 = o12_ref[:BQ, :LANES] / o12_ref[:BQ, LANES:][:, ONE : ONE + 1]
        o2a, o2b = o12_ref[BQ:, :LANES], o12_ref[BQ:, LANES:]
        t2 = o2b[:, ONE : ONE + 1]
        o2a, o2b = o2a / t2, o2b / t2
        out_ref[b, :OWN, :] = jnp.where(lane < HD, o0, o2a).astype(jnp.bfloat16)
        out_ref[b, OWN : 2 * OWN, :] = jnp.where(lane < HD, o1, turned(o2b, 96)).astype(jnp.bfloat16)
        part = OWN // 4
        lane = lane_iota((part, LANES))
        fold = turned(o2b[:part], 96)
        for g in range(1, 4):
            fold = jnp.where(lane < 32 * g, fold, turned(o2b[g * part : (g + 1) * part], 32 * g - 32))
        out_ref[b, 2 * OWN :, :] = fold.astype(jnp.bfloat16)
        return carry

    lax.fori_loop(0, GROUP, block, 0)


def attend(prev, own, following, queries, seg_rows):
    vmem = pl.BlockSpec(memory_space=pltpu.VMEM)
    return pl.pallas_call(
        attend_kernel,
        out_shape=jax.ShapeDtypeStruct((GROUP, OUT_ROWS, LANES), jnp.bfloat16),
        in_specs=[vmem] * 5,
        out_specs=vmem,
        scratch_shapes=[
            pltpu.VMEM((WINDOW, KV_LANES), jnp.bfloat16),
            pltpu.VMEM((WINDOW, LANES), jnp.bfloat16),
            pltpu.VMEM((3, SHARD, LANES), jnp.bfloat16),
            pltpu.VMEM((SHARD, LANES), jnp.bfloat16),
            pltpu.VMEM((MAX_BLOCKS, 3, BQ, BK), jnp.float32),
            pltpu.VMEM((3, BQ, LANES), jnp.float32),
            pltpu.VMEM((BQ, LANES), jnp.float32),
            pltpu.VMEM((2 * BQ, 2 * LANES), jnp.float32),
            pltpu.SMEM((GROUP,), jnp.int32),
            pltpu.SMEM((GROUP,), jnp.int32),
        ],
        compiler_params=pltpu.CompilerParams(vmem_limit_bytes=40 * 1024 * 1024),
        name="attend",
    )(prev, own, following, queries, seg_rows)


def unpack_kernel(in_ref, out_ref):
    lane = lane_iota((OWN, LANES))
    part = OWN // 4

    def source(z, i):
        if i < 3:
            return in_ref[z, :OWN, :], i
        if i < 6:
            return in_ref[z, OWN : 2 * OWN, :], i - 3
        return in_ref[z, (i - 6) * OWN : (i - 5) * OWN, :], 3

    for t in range(D // LANES):
        value = None
        for g in range(4):
            z, i = divmod(4 * t + g, 9)
            if i == 8:
                pieces = [turned(in_ref[z, 2 * OWN :, :], 32 * (g - p)) for p in range(4)]
                moved = jnp.concatenate(pieces, axis=0)
            else:
                tile, at = source(z, i)
                moved = turned(tile, 32 * (g - at))
            value = moved if value is None else jnp.where(lane < 32 * g, value, moved)
        out_ref[:, t * LANES : (t + 1) * LANES] = value


def unpack(returned):
    vmem = pl.BlockSpec(memory_space=pltpu.VMEM)
    return pl.pallas_call(
        unpack_kernel,
        out_shape=jax.ShapeDtypeStruct((OWN, D), jnp.bfloat16),
        in_specs=[vmem],
        out_specs=vmem,
        compiler_params=pltpu.CompilerParams(vmem_limit_bytes=32 * 1024 * 1024),
        name="unpack",
    )(returned)


def frequencies():
    quarter = HD // 4
    lane = np.arange(LANES)
    return (10000.0 ** (-(lane % quarter).astype(np.float64) / quarter)).astype(np.float32)[None, :]


def body(projected, segment_ids, widths):
    seg_rows = segment_ids.reshape(SEG_ROWS, LANES)
    widths_row = jnp.pad(widths, (0, LANES - SAMPLES)).reshape(1, LANES)
    kv, q = pack(projected, seg_rows, widths_row, jnp.asarray(frequencies()))
    kv = lax.all_to_all(kv, "head", 0, 0, tiled=True)
    kv, q = lax.optimization_barrier((kv, q))
    own = kv.reshape(SHARD, KV_LANES)
    up = [(i, (i + 1) % SEQ) for i in range(SEQ)]
    down = [(j, i) for i, j in up]
    prev = lax.ppermute(own, "seq", up)
    following = lax.ppermute(own, "seq", down)
    q = lax.all_to_all(q, "head", 0, 0, tiled=True)
    out = attend(prev, own, following, q.reshape(SHARD, Q_LANES), seg_rows)
    out = lax.all_to_all(out, "head", 0, 0, tiled=True)
    return unpack(out)


def solution(mesh):
    in_specs = (P(("seq", "head"), None), P(), P())
    out_specs = P(("seq", "head"), None)
    return jax.shard_map(body, mesh=mesh, in_specs=in_specs, out_specs=out_specs, check_vma=False)
```

time: 287 us -> 174 us (0.61)
  matrix products: 64.6 us -> 0 us
  Pallas kernels: 0 us -> 58.8 us
  other arithmetic: 34.4 us -> 0 us
  blocking collectives: 134 us -> 108 us
  local copies, waits for them, and re-layouts: 28.2 us -> 3.99 us
  waiting for transfers between devices: 15.6 us -> 0.01 us
  starting transfers between devices: 5.56 us -> 0.51 us
    dot_general x18 -> x0, matrix products: 64.6 us -> none  [the longest x9 48.1 us: block_scores(): lax.dot_general(q_rows, k_rows, (((1,), (1,)), ((), ())), preferred_eleme...]
    pallas_call x0 -> x3, Pallas kernels: none -> 58.8 us  [the longest x1 40.3 us: attend(): pl.pallas_call(attend_kernel, out_shape=jax.ShapeDtypeStruct((GROUP, OUT_...]
    reduce_sum x4 -> x0, other arithmetic: 25.6 us -> none  [the longest x3 25.5 us: dense_rows(): totals = jnp.sum(weights, axis=1, keepdims=True)]
    all_to_all x2 -> x3, blocking collectives: 134 us -> 108 us  [the longest x1 56.8 us: body(): kv = lax.all_to_all(kv, 'head', 0, 0, tiled=True)]
    ppermute x2, waiting for transfers between devices: 15.6 us -> 0.01 us  [the longest x1 0.01 us: body(): following = lax.ppermute(own, 'seq', down)]
    all_to_all x3 -> x0, local copies, waits for them, and re-layouts: 7.22 us -> none  [the longest x2 6.32 us: body(): lax.all_to_all(stacked, 'head', split_axis=2, concat_axis=0, tiled=True)]
    ppermute x2, starting transfers between devices: 5.56 us -> 0.51 us  [the longest x1 0.51 us: body(): prev = lax.ppermute(own, 'seq', up)]
    squeeze x2 -> x0, local copies, waits for them, and re-layouts: 3.99 us -> none  [the longest x1 2.16 us: body(): qkv_part[:, 0, 0]]
  transfers between devices with their start and end apart: 2 -> 2, of which waited for: 2 -> 0; matrix products, arithmetic and copies ran while one was open for 2% -> 0% of each run, Pallas kernels for 0% -> 0%
where the time goes in v1:
time: 174 us; the launch traced here: 172 us
  blocking collectives  108 us (62%)
  Pallas kernels  58.8 us (34%)
  local copies, waits for them, and re-layouts  3.99 us (2%)
    all_to_all x1, blocking collectives, body(): kv = lax.all_to_all(kv, 'head', 0, 0, tiled=True)  56.8 us
    pallas_call x1, Pallas kernels, attend(): pl.pallas_call(attend_kernel, out_shape=jax.ShapeDtypeStruct((GROUP, OUT_...  40.3 us
    all_to_all x1, blocking collectives, body(): q = lax.all_to_all(q, 'head', 0, 0, tiled=True)  26.8 us
    all_to_all x1, blocking collectives, body(): out = lax.all_to_all(out, 'head', 0, 0, tiled=True)  24.7 us
    pallas_call x1, Pallas kernels, pack(): pl.pallas_call(pack_kernel, out_shape=[jax.ShapeDtypeStruct((GROUP, OWN,...  17 us
  transfers between devices with their start and end apart: 2, of which 0 were waited for; matrix products, arithmetic and copies ran while one was open for 0% of the time, Pallas kernels for 0%

profile of v1, /device:TPU:20, one launch (start us, length us, event | category | flops | bytes accessed | tf_op | source)
XLA Modules:
  0.0 171.7 jit_solution(4810338515782442741)
XLA Ops:
  0.0 0.7 pad_bitcast_fusion.widths_ref
  0.7 0.0 copy-start
  0.7 1.7 %copy-done = bf16[192,6912]{1,0:T(8,128)(2,1)S(1)} copy-done((bf16[192,6912]{1,0:T(8,128)(2,1)S(1)}, bf16[192,6912]{1,0:T(8,128)(2,1)}, u32[]{:S(2)}) %copy-start) | copy-done | bytes 2654232
  2.4 0.0 copy-start.1
  2.4 0.9 copy-done.1
  3.3 0.0 copy-start.3
  3.3 0.7 copy-done.3
  4.0 17.0 %pack.1 = (bf16[8,192,640]{2,1,0:T(8,128)(2,1)S(1)}, bf16[8,192,256]{2,1,0:T(8,128)(2,1)S(1)}) custom-call(bf16[192,6912]{1,0:T(8,128)(2,1)S(1)} %copy-done, s32[384,128]{1,0:T(8,128)S(1)} %bitcast.9, s32[1,128]{1,0:T(1,128)S(1)} %pad_bitcast_fusion.widths_ref, f32[1,128]{1,0:T(1,128)S(1)} %copy-done.3), custom_call_target="tpu_custom_call" | custom-call | tf_op jit(solution)/shard_map/pack/pallas_call | solution.py:129
  21.0 0.0 copy-start.2
  21.0 56.8 %all_to_all.15 = bf16[8,192,640]{2,1,0:T(8,128)(2,1)S(1)} all-to-all(bf16[8,192,640]{2,1,0:T(8,128)(2,1)S(1)} %get-tuple-element.9), channel_id=1, replica_groups=mesh['seq'=32,'head'=8] {'head'}, dimensions={0} | all-to-all | bytes 3932160 | tf_op jit(solution)/shard_map/all_to_all | solution.py:348
  77.8 0.0 collective-permute-start.1
  77.8 0.5 collective-permute-start
  78.3 26.8 %all_to_all.16 = bf16[8,192,256]{2,1,0:T(8,128)(2,1)S(1)} all-to-all(bf16[8,192,256]{2,1,0:T(8,128)(2,1)S(1)} %get-tuple-element.12), channel_id=1, replica_groups=mesh['seq'=32,'head'=8] {'head'}, dimensions={0} | all-to-all | bytes 1572864 | tf_op jit(solution)/shard_map/all_to_all | solution.py:355
  105.1 0.0 collective-permute-done.1.next_ref
  105.1 0.0 collective-permute-done.prev_ref
  105.1 0.0 copy-done.2
  105.1 40.3 %attend.1 = bf16[8,432,128]{2,1,0:T(8,128)(2,1)S(1)} custom-call(bf16[1536,640]{1,0:T(8,128)(2,1)S(1)} %collective-permute-done.prev_ref, bf16[1536,640]{1,0:T(8,128)(2,1)S(1)} %bitcast.7, bf16[1536,640]{1,0:T(8,128)(2,1)S(1)} %collective-permute-done.1.next_ref, bf16[1536,256]{1,0:T(8,128)(2,1)S(1)} %bitcast.8, s32[384,128]{1,0:T(8,128)S(1)} %bitcast.10), custom_call_target="tpu_custom_call" | custom-call | tf_op jit(solution)/shard_map/attend/pallas_call | solution.py:279
  145.5 24.7 %all_to_all.17.in_ref = bf16[8,432,128]{2,1,0:T(8,128)(2,1)S(1)} all-to-all(bf16[8,432,128]{2,1,0:T(8,128)(2,1)S(1)} %attend.1), channel_id=1, replica_groups=mesh['seq'=32,'head'=8] {'head'}, dimensions={0} | all-to-all | bytes 1769472 | tf_op jit(solution)/shard_map/all_to_all | solution.py:357
  170.2 1.5 unpack.1
Async XLA Ops:
  0.7 1.7 %copy-start = (bf16[192,6912]{1,0:T(8,128)(2,1)S(1)}, bf16[192,6912]{1,0:T(8,128)(2,1)}, u32[]{:S(2)}) copy-start(bf16[192,6912]{1,0:T(8,128)(2,1)} %x_ref.1) | copy-start | bytes 7962628
  2.4 0.9 copy-start.1
  3.3 0.7 copy-start.3
  21.0 84.2 %copy-start.2 = (s32[49152]{0:T(1024)S(1)}, s32[49152]{0:T(1024)}, u32[]{:S(2)}) copy-start(s32[49152]{0:T(1024)} %param.5) | copy-start | bytes 589828
  77.8 27.4 %collective-permute-start.1 = (bf16[1536,640]{1,0:T(8,128)(2,1)S(1)}, bf16[1536,640]{1,0:T(8,128)(2,1)S(1)}, u32[]{:S(2)}, u32[]{:S(2)}) collective-permute-start(bf16[1536,640]{1,0:T(8,128)(2,1)S(1)} %bitcast.5), channel_id=1, source_target_pairs={{8,0},{16,8},{24,16},{32,24},{40,32},{48,40},{56,48},{64,56},{72,6... | collective-permute-start | bytes 5898248 | tf_op jit(solution)/shard_map/ppermute | solution.py:354
  77.8 27.4 %collective-permute-start = (bf16[1536,640]{1,0:T(8,128)(2,1)S(1)}, bf16[1536,640]{1,0:T(8,128)(2,1)S(1)}, u32[]{:S(2)}, u32[]{:S(2)}) collective-permute-start(bf16[1536,640]{1,0:T(8,128)(2,1)S(1)} %bitcast.6), channel_id=1, source_target_pairs={{0,8},{8,16},{16,24},{24,32},{32,40},{40,48},{48,56},{56,64},{64,7... | collective-permute-start | bytes 5898248 | tf_op jit(solution)/shard_map/ppermute | solution.py:353
